TPU v7x, 512 devices: a whole 4x4x16 slice. The times are simulated.
512 devices in a mesh: blk: 128 (over y, z_lo, x, core), head: 4 (over z_hi).
Axes of the slice: x: 4, y: 4, z: 16 (z_hi: 4, z_lo: 4; z = z_hi * 4 + z_lo), core: 2. Of those that a mesh axis runs over, the one named last changes fastest.
Arguments:
- query_states: bfloat16 [128, 2, 64, 2048], P('blk', None, 'head'), may hold values from -24 to 24
- key_states: bfloat16 [128, 2, 64, 512], P('blk', None, None, 'head'), may hold values from -6 to 6
- value_states: bfloat16 [128, 2, 64, 512], P('blk', None, None, 'head'), may hold values from -6 to 6
- doc_lengths: int32 [3], replicated, may hold values from 1 to 12288, 16384 in all
- page_slot: int32 [128, 2, 4], replicated, may hold values from 0 to 2047, as said below
Outputs:
- attended: bfloat16 [128, 2, 64, 2048], P('blk', None, None, 'head')
- kv_cache: bfloat16 [2048, 4, 16, 256], P('blk', 'head')
Inputs may be any that keep to these rules, and one draw needn't show every extreme that they name: `page_slot`: all entries differ. The busiest owners hold 16 pages, the least busy 4.
All inputs are finite; a program needn't handle non-finite values.
Results may differ from a plain program's by a relative error of at most 0.007.
Values may be sent and summed in bfloat16 or wider, within the bound.
A program may use at most 64 MiB of HBM per device.

v0:
```python
import jax
import jax.numpy as jnp
from jax import lax
from jax.sharding import PartitionSpec as P

PAGE = 16


def per_device(query_states, key_states, value_states, doc_lengths, page_slot):
    q_local = lax.all_to_all(query_states, "head", split_axis=3, concat_axis=2, tiled=True)
    axis_count = lax.axis_size("blk")
    my_index = lax.axis_index("blk")
    block_tok = q_local.shape[2]
    head_dim = key_states.shape[3]
    group_size = q_local.shape[3] // head_dim
    query_rows = q_local.reshape(2 * block_tok, group_size, head_dim)
    offsets = jnp.arange(block_tok, dtype=jnp.int32)
    doc_bounds = jnp.cumsum(doc_lengths)[:-1]
    page_count = block_tok // PAGE
    slot_count = 4 * page_count
    slot_range = jnp.arange(slot_count, dtype=jnp.int32)
    score_scale = head_dim ** (-0.5)

    def group_positions(owner_ids):
        block_starts = jnp.stack([owner_ids, 2 * axis_count - 1 - owner_ids], axis=1) * block_tok
        return (block_starts[:, :, None] + offsets[None, None, :]).reshape(-1)

    def doc_of(positions):
        return jnp.sum((positions[:, None] >= doc_bounds[None, :]).astype(jnp.int32), axis=1)

    q_pos = group_positions(my_index.reshape(1))
    q_doc = doc_of(q_pos)

    def attend_group(attn_state, key_rows, value_rows, allowed):
        running_max, weight_sum, accum = attn_state
        scores = (
            jnp.einsum("qhd,kd->qhk", query_rows, key_rows, preferred_element_type=jnp.float32)
            * score_scale
        )
        masked = jnp.where(allowed[:, None, :], scores, -1e30)
        new_max = jnp.maximum(running_max, jnp.max(masked, axis=2))
        weights = jnp.where(allowed[:, None, :], jnp.exp(masked - new_max[..., None]), 0.0)
        factor = jnp.exp(running_max - new_max)
        weight_sum = weight_sum * factor + jnp.sum(weights, axis=2)
        update = jnp.einsum(
            "qhk,kd->qhd",
            weights.astype(jnp.bfloat16),
            value_rows,
            preferred_element_type=jnp.float32,
        )
        accum = accum * factor[..., None] + update
        return (new_max, weight_sum, accum)

    def visit_group(attn_state, key_group, value_group, owner_ids):
        key_rows = key_group.reshape(-1, head_dim)
        value_rows = value_group.reshape(-1, head_dim)
        k_pos = group_positions(owner_ids)
        allowed = (k_pos[None, :] <= q_pos[:, None]) & (doc_of(k_pos)[None, :] == q_doc[:, None])
        return attend_group(attn_state, key_rows, value_rows, allowed)

    def place_pages(page_store, key_group, value_group, owner_ids):
        page_rows = jnp.concatenate([key_group, value_group], axis=-1).reshape(
            -1, PAGE * 2 * head_dim
        )
        slot_ids = jnp.take(page_slot, owner_ids, axis=0).reshape(-1) - my_index * slot_count
        selector = (slot_range[:, None] == slot_ids[None, :]).astype(jnp.bfloat16)
        return page_store + jnp.dot(selector, page_rows, preferred_element_type=jnp.float32)

    def fold_groups(step_fn, carried, kv_piece):
        key_piece, value_piece = kv_piece
        piece_len = key_piece.shape[0]
        width = 4
        owner_ids = jnp.arange(piece_len, dtype=jnp.int32).reshape(piece_len // width, width)
        key_groups = key_piece.reshape(piece_len // width, width, 2, block_tok, head_dim)
        value_groups = value_piece.reshape(piece_len // width, width, 2, block_tok, head_dim)

        def visit_one(inner_state, entry_tuple):
            key_group, value_group, owners = entry_tuple
            return (step_fn(inner_state, key_group, value_group, owners), None)

        return lax.scan(visit_one, carried, (key_groups, value_groups, owner_ids))[0]

    empty_store = jnp.zeros((slot_count, PAGE * 2 * head_dim), jnp.float32)
    start_state = (
        jnp.full((2 * block_tok, group_size), -1e30, jnp.float32),
        jnp.zeros((2 * block_tok, group_size), jnp.float32),
        jnp.zeros((2 * block_tok, group_size, head_dim), jnp.float32),
    )
    final_state = fold_groups(
        visit_group,
        start_state,
        (
            lax.all_gather(key_states, "blk", axis=0, tiled=True),
            lax.all_gather(value_states, "blk", axis=0, tiled=True),
        ),
    )
    page_store = fold_groups(
        place_pages,
        empty_store,
        (
            lax.all_gather(key_states, "blk", axis=0, tiled=True),
            lax.all_gather(value_states, "blk", axis=0, tiled=True),
        ),
    )
    running_max, weight_sum, accum = final_state
    attended = (
        (accum / weight_sum[..., None])
        .astype(jnp.bfloat16)
        .reshape(1, 2, block_tok, group_size * head_dim)
    )
    kv_cache = page_store.astype(jnp.bfloat16).reshape(slot_count, 1, PAGE, 2 * head_dim)
    return (attended, kv_cache)


def solution(mesh):
    return jax.shard_map(
        per_device,
        mesh=mesh,
        in_specs=(
            P("blk", None, "head", None),
            P("blk", None, None, "head"),
            P("blk", None, None, "head"),
            P(),
            P(),
        ),
        out_specs=(P("blk", None, None, "head"), P("blk", "head", None, None)),
        check_vma=False,
    )
```

profile of v0, /device:TPU:1, one launch (start us, length us, event | category | flops | bytes accessed | tf_op | source)
XLA Modules:
  0.0 593.8 jit_solution(2853987302329961732)
XLA Ops:
  8.6 2.0 copy.26
  10.7 1.7 reshape.326
  12.4 15.6 %all-to-all-start = ((bf16[4,2,8192]{2,1,0:T(2,128)(2,1)}), bf16[4,2,8192]{2,1,0:T(2,128)(2,1)S(1)}, u32[]{:S(2)}, u32[]{:S(2)}) async-start(bf16[4,2,8192]{2,1,0:T(2,128)(2,1)} %reshape.326), calls=%async_computation | async-start | bytes 262144 | tf_op jit(solution)/shard_map/all_to_all | solution.py:10
  30.2 10.6 %all-to-all-done = bf16[4,2,8192]{2,1,0:T(2,128)(2,1)S(1)} async-done(((bf16[4,2,8192]{2,1,0:T(2,128)(2,1)}), bf16[4,2,8192]{2,1,0:T(2,128)(2,1)S(1)}, u32[]{:S(2)}, u32[]{:S(2)}) %all-to-all-start) | async-done | bytes 131104 | tf_op jit(solution)/shard_map/all_to_all | solution.py:10
  42.1 178.9 %all-gather.3.cloned.1.call-done = bf16[128,2,64,128]{3,2,1,0:T(8,128)(2,1)} async-done(((bf16[1,2,64,128]{3,2,1,0:T(8,128)(2,1)}), bf16[128,2,64,128]{3,2,1,0:T(8,128)(2,1)}) %all-gather.3.cloned.1.call-update) | async-done | bytes 4194320 | tf_op jit(solution)/shard_map/all_gather | solution.py:93
  221.1 205.9 %all-gather.5.cloned.1.call-done = bf16[128,2,64,128]{3,2,1,0:T(8,128)(2,1)} async-done(((bf16[1,2,64,128]{3,2,1,0:T(8,128)(2,1)}), bf16[128,2,64,128]{3,2,1,0:T(8,128)(2,1)}) %all-gather.5.cloned.1.call-update) | async-done | bytes 4194320 | tf_op jit(solution)/shard_map/all_gather | solution.py:94
  427.0 88.9 %while.28 = (s32[]{:T(128)}, f32[128,4]{0,1:T(4,128)S(1)}, f32[128,4]{0,1:T(4,128)S(1)}, f32[128,4,128]{2,0,1:T(8,128)S(1)}, s32[32,4]{1,0:T(8,128)S(1)}, /*inde...) while((s32[]{:T(128)}, f32[128,4]{0,1:T(4,128)S(1)}, ...), condition=%wide.region_6.7_spmd.clone, body=%wide.region_2.6_spmd.clone.sunk | while | flops 136976032 | bytes 4899697 | solution.py:81
  427.8 1.0 constant_dynamic-slice_fusion.5
  430.5 1.0 constant_dynamic-slice_fusion.5
  433.3 1.0 constant_dynamic-slice_fusion.5
  436.1 1.0 constant_dynamic-slice_fusion.5
  438.9 1.0 constant_dynamic-slice_fusion.5
  441.7 1.0 constant_dynamic-slice_fusion.5
  444.4 1.0 constant_dynamic-slice_fusion.5
  447.2 1.0 constant_dynamic-slice_fusion.5
  450.0 1.0 constant_dynamic-slice_fusion.5
  452.8 1.0 constant_dynamic-slice_fusion.5
  455.6 1.0 constant_dynamic-slice_fusion.5
  458.3 1.0 constant_dynamic-slice_fusion.5
  461.1 1.0 constant_dynamic-slice_fusion.5
  463.9 1.0 constant_dynamic-slice_fusion.5
  466.7 1.0 constant_dynamic-slice_fusion.5
  469.4 1.0 constant_dynamic-slice_fusion.5
  472.2 1.0 constant_dynamic-slice_fusion.5
  475.0 1.0 constant_dynamic-slice_fusion.5
  477.8 1.0 constant_dynamic-slice_fusion.5
  480.6 1.0 constant_dynamic-slice_fusion.5
  483.3 1.0 constant_dynamic-slice_fusion.5
  486.1 1.0 constant_dynamic-slice_fusion.5
  488.9 1.0 constant_dynamic-slice_fusion.5
  491.7 1.0 constant_dynamic-slice_fusion.5
  494.5 1.0 constant_dynamic-slice_fusion.5
  497.2 1.0 constant_dynamic-slice_fusion.5
  500.0 1.0 constant_dynamic-slice_fusion.5
  502.8 1.0 constant_dynamic-slice_fusion.5
  505.6 1.0 constant_dynamic-slice_fusion.5
  508.4 1.0 constant_dynamic-slice_fusion.5
  511.1 1.0 constant_dynamic-slice_fusion.5
  513.9 1.0 constant_dynamic-slice_fusion.5
  516.9 69.3 %while.29 = (s32[]{:T(128)}, f32[16,4096]{1,0:T(8,128)S(1)}, s32[32,4]{1,0:T(8,128)S(1)}, s32[128,2,4]{2,1,0:T(2,128)S(1)}, s32[]{:T(128)}, /*index=5*/bf16[32,4...) while((s32[]{:T(128)}, f32[16,4096]{1,0:T(8,128)S(1)}, ...), condition=%wide.region_8.9_spmd.clone, body=%wide.region_7.8_spmd.clone.sunk | while | flops 4851303 | bytes 2364495 | solution.py:81
  521.2 1.0 dynamic-slice_bitcast_fusion.3
  525.6 1.0 dynamic-slice_bitcast_fusion.3
  532.1 1.0 dynamic-slice_bitcast_fusion.3
  536.4 1.0 dynamic-slice_bitcast_fusion.3
  542.9 1.0 dynamic-slice_bitcast_fusion.3
  547.2 1.0 dynamic-slice_bitcast_fusion.3
  553.7 1.0 dynamic-slice_bitcast_fusion.3
  560.2 1.0 dynamic-slice_bitcast_fusion.3
  (820 shorter events, 120.6 us)
Async XLA Ops:
  7.2 213.9 %all-gather.3.cloned.1.call-start = ((), (), s32[]{:S(2)}) async-start(), calls=%async_computation.1 | async-start | bytes 4227072 | tf_op jit(solution)/shard_map/all_gather | solution.py:93
  7.9 419.1 %all-gather.5.cloned.1.call-start = ((), (), s32[]{:S(2)}) async-start(), calls=%async_computation.2 | async-start | bytes 4227072 | tf_op jit(solution)/shard_map/all_gather | solution.py:94
  12.4 28.3 %all-to-all-start = ((bf16[4,2,8192]{2,1,0:T(2,128)(2,1)}), bf16[4,2,8192]{2,1,0:T(2,128)(2,1)S(1)}, u32[]{:S(2)}, u32[]{:S(2)}) async-start(bf16[4,2,8192]{2,1,0:T(2,128)(2,1)} %reshape.326), calls=%async_computation | async-start | bytes 262144 | tf_op jit(solution)/shard_map/all_to_all | solution.py:10
Sparse Core Ops, SparseCore 0:
  10.2 210.8 all-gather.2
  223.2 203.7 all-gather.4
where the time goes:
time: 595 us; the launch traced here: 594 us
  waiting for transfers between devices  397 us (67%)
  local copies, waits for them, and re-layouts  105 us (18%)
  matrix products  30.2 us (5%)
  other arithmetic  27.7 us (5%)
  starting transfers between devices  15.7 us (3%)
  between operations  14.1 us (2%)
    all_gather x1, waiting for transfers between devices, per_device(): lax.all_gather(value_states, 'blk', axis=0, tiled=True)  206 us
    all_gather x1, waiting for transfers between devices, per_device(): lax.all_gather(key_states, 'blk', axis=0, tiled=True)  179 us
    dynamic_slice x32, local copies, waits for them, and re-layouts, fold_groups(): lax.scan(visit_one, carried, (key_groups, value_groups, owner_ids))[0]  31.8 us
    squeeze x32, local copies, waits for them, and re-layouts, fold_groups(): lax.scan(visit_one, carried, (key_groups, value_groups, owner_ids))[0]  31.7 us
    gather x32, local copies, waits for them, and re-layouts, place_pages(): jnp.take(page_slot, owner_ids, axis=0).reshape(-1) - my_index * slot_count  18.3 us
    all_to_all x1, starting transfers between devices, per_device(): lax.all_to_all(query_states, 'head', split_axis=3, concat_axis=2, tiled=T...  15.6 us
    dot_general x32, matrix products, attend_group(): jnp.einsum('qhk,kd->qhd', weights.astype(jnp.bfloat16), value_rows, prefe...  14.1 us
  transfers between devices with their start and end apart: 3, of which 3 were waited for; matrix products, arithmetic and copies ran while one was open for 1% of the time, Pallas kernels for 0%

commit v1 on v0

v1 whole, which is shorter than its diff:
```python
import functools
import jax
import jax.numpy as jnp
from jax import lax
from jax.experimental import pallas as pl
from jax.experimental.pallas import tpu as pltpu
from jax.sharding import PartitionSpec as P

MESH = pl.DeviceIdType.MESH
PAGE = 16
NEG = -1e30
LAG = 4


def order(k):
    return k + k // 2 - 2 * (k // 3)


def kernel(
    q_ref, k_ref, v_ref, doc_ref, slot_ref, out_ref, cache_ref,
    buf, qbuf, qrow, start, qpos, m_s, l_s, acc_s, pages,
    z_recv, a_recv, b_recv, f_recv, d_recv, q_recv, z_send, a_send, b_send, f_send, d_send, q_send,
):
    blk = lax.axis_index("blk")
    head = lax.axis_index("head")
    y, z, x, c = blk // 32, (blk // 8) % 4, (blk // 2) % 4, blk % 2

    def device(yy, zz, xx, cc):
        return (((yy * 4 + zz) * 4 + xx) * 2 + cc, head)

    sibling = device(y, z, x, 1 - c)
    z_peers = [z + 1 - 2 * (z % 2), (z + 2) % 4, 3 - z]

    def remote(src, dst, send, recv, dev):
        return pltpu.make_async_remote_copy(
            src_ref=src, dst_ref=dst, send_sem=send, recv_sem=recv, device_id=dev, device_id_type=MESH
        )

    for half in range(2):
        buf[half, c, y, x, z, 0] = k_ref[0, half].reshape(4, PAGE, 128)
        buf[half, c, y, x, z, 1] = v_ref[0, half].reshape(4, PAGE, 128)

    barrier = pltpu.get_barrier_semaphore()
    peers = [sibling]
    for d in range(1, 4):
        peers.append(device(y, z_peers[d - 1], x, c))
        peers.append(device(y, z, (x + d) % 4, c))
        peers.append(device((y + d) % 4, z, x, c))
        peers.append((blk, (head + d) % 4))
    for dev in peers:
        pl.semaphore_signal(barrier, inc=1, device_id=dev, device_id_type=MESH)
    pl.semaphore_wait(barrier, len(peers))

    for d in range(3):
        unit = buf.at[:, c, y, x, z]
        remote(unit, unit, z_send, z_recv.at[d], device(y, z_peers[d], x, c)).start()

    def send_first(zz):
        for d in (1, 3, 2):
            low = buf.at[0, c, y, x, zz]
            remote(low, low, a_send, a_recv.at[0, d - 1], device(y, z, (x + d) % 4, c)).start()
            high = buf.at[1, c, y, x, zz]
            remote(high, high, a_send, a_recv.at[1, d - 1], device((y + d) % 4, z, x, c)).start()

    send_first(z)

    def query_copy(d):
        to = (head + d) % 4
        return remote(
            q_ref.at[0, :, :, pl.ds(pl.multiple_of(to * 512, 512), 512)],
            qbuf.at[:, pl.ds(pl.multiple_of(head * 16, 16), 16), :],
            q_send, q_recv.at[d - 1], (blk, to),
        )

    for d in range(1, 4):
        query_copy(d).start()
    qbuf[:, pl.ds(pl.multiple_of(head * 16, 16), 16), :] = q_ref[0, :, :, pl.ds(pl.multiple_of(head * 512, 512), 512)]

    bound0 = doc_ref[0]
    bound1 = doc_ref[0] + doc_ref[1]
    for qb in range(2):
        row = lax.broadcasted_iota(jnp.int32, (256, 128), 0) % 64
        pos = row + (blk if qb == 0 else 255 - blk) * 64
        qpos[qb] = pos
        start[qb] = jnp.where(pos >= bound1, bound1, jnp.where(pos >= bound0, bound0, 0))
    m_s[...] = jnp.full_like(m_s, NEG)
    l_s[...] = jnp.zeros_like(l_s)
    acc_s[...] = jnp.zeros_like(acc_s)

    for d in range(3):
        unit = buf.at[:, c, y, x, z_peers[d]]
        remote(unit, unit, z_send, z_recv.at[d], device(y, z_peers[d], x, c)).wait_recv()
        send_first(z_peers[d])

    local = slot_ref[...] - blk * 16
    ident = (
        lax.broadcasted_iota(jnp.int32, local.shape, 0) * 8
        + lax.broadcasted_iota(jnp.int32, local.shape, 1) * 4
        + lax.broadcasted_iota(jnp.int32, local.shape, 2)
        + 1
    )
    for s in range(16):
        pages[s] = jnp.max(jnp.where(local == s, ident, 0))

    def group(g):
        half, p = g % 2, g // 2
        stage = p // 4
        both = (stage + 1) // 2 - 2 * (stage // 3)
        k = (1 - both) * (p % 4) + both * ((p + 12) // 2 - 8)
        b_off = both * (2 * (p % 2) - 1) + 2 * (stage // 3)
        return half, k, order(k), b_off

    def place(half, a_off, b_off):
        yy = (y + 8 + (1 - half) * b_off + half * a_off) % 4
        xx = (x + 8 + half * b_off + (1 - half) * a_off) % 4
        return yy, xx

    def to_sibling(g, half, yy, xx):
        column = buf.at[half, c, yy, xx]
        remote(column, column, d_send, d_recv.at[g], sibling).start()

    scale = 128 ** -0.5 * 1.4426950408889634

    def attend(qb, half, yy, xx):
        keys = buf[half, :, yy, xx, :, 0].reshape(512, 128)
        values = buf[half, :, yy, xx, :, 1].reshape(512, 128)
        scores = lax.dot_general(qrow[qb], keys, (((1,), (1,)), ((), ())), preferred_element_type=jnp.float32)
        lo, hi = start[qb], qpos[qb]
        sign = 1 - 2 * half
        first = half * 255 + sign * (32 * yy + 2 * xx)
        lane = lax.broadcasted_iota(jnp.int32, (1, 128), 1)
        parts = []
        for t in range(4):
            unit = (t // 2) + 8 * (2 * (t % 2) + lane // 64)
            k_pos = (first + sign * unit) * 64 + lane % 64
            part = scores[:, 128 * t : 128 * (t + 1)]
            parts.append(jnp.where((k_pos >= lo) & (k_pos <= hi), part, NEG))
        top = jnp.maximum(jnp.maximum(parts[0], parts[1]), jnp.maximum(parts[2], parts[3]))
        old = m_s[qb]
        new = jnp.maximum(old, jnp.max(top, axis=1, keepdims=True))
        m_s[qb] = new
        factor = jnp.exp2((old - new) * scale)
        weights = [jnp.exp2((part - new) * scale) for part in parts]
        l_s[qb] = l_s[qb] * factor + ((weights[0] + weights[1]) + (weights[2] + weights[3]))
        rounded = jnp.concatenate([w.astype(jnp.bfloat16) for w in weights], axis=1)
        acc_s[qb] = acc_s[qb] * factor + jnp.dot(rounded, values, preferred_element_type=jnp.float32)

    def compute(g):
        half, _, a_off, b_off = group(g)
        yy, xx = place(half, a_off, b_off)
        column = buf.at[half, 1 - c, yy, xx]
        remote(column, column, d_send, d_recv.at[g], sibling).wait_recv()

        @pl.when((half == 0) | (yy >= y))
        def _():
            attend(1, half, yy, xx)

        @pl.when((half == 0) & (yy <= y))
        def _():
            attend(0, half, yy, xx)

    def second_device(half, step):
        yy, xx = place(half, 0, step)
        return device(yy, z, xx, c)

    def first_steps(g, _):
        half, k, a_off, b_off = group(g)
        yy, xx = place(half, a_off, b_off)
        column = buf.at[half, c, yy, xx]

        @pl.when(g >= 2)
        def _():
            remote(column, column, a_send, a_recv.at[half, 3 - a_off], sibling).wait_recv()

        for direction in range(2):
            remote(
                column, column, b_send, b_recv.at[half, k, direction], second_device(half, 1 - 2 * direction)
            ).start()
        to_sibling(g, half, yy, xx)

        @pl.when(g == 1)
        def _():
            for d in range(1, 4):
                query_copy(d).wait_recv()
            for qb in range(2):
                for h in range(4):
                    qrow[qb, 64 * h : 64 * (h + 1)] = qbuf[qb, :, 128 * h : 128 * (h + 1)]

        @pl.when(g >= LAG)
        def _():
            compute(g - LAG)

        return 0

    def second_steps(g, _):
        half, k, a_off, b_off = group(g)
        yy, xx = place(half, a_off, b_off)
        direction = (b_off + 1) // 2
        column = buf.at[half, c, yy, xx]
        remote(column, column, b_send, b_recv.at[half, k, direction], sibling).wait_recv()
        piece = buf.at[half, c, yy, xx, :, direction]
        remote(piece, piece, f_send, f_recv.at[half, k, direction], second_device(half, 1 - 2 * direction)).start()
        to_sibling(g, half, yy, xx)
        compute(g - LAG)
        return 0

    def third_steps(g, _):
        half, k, a_off, b_off = group(g)
        yy, xx = place(half, a_off, b_off)
        for direction in range(2):
            piece = buf.at[half, c, yy, xx, :, direction]
            remote(piece, piece, f_send, f_recv.at[half, k, direction], sibling).wait_recv()
        to_sibling(g, half, yy, xx)
        compute(g - LAG)
        return 0

    def last_steps(g, _):
        compute(g)
        return 0

    lax.fori_loop(0, 8, first_steps, 0)
    lax.fori_loop(8, 24, second_steps, 0)
    lax.fori_loop(24, 32, third_steps, 0)
    lax.fori_loop(32 - LAG, 32, last_steps, 0)

    for qb in range(2):
        for h in range(4):
            rows = slice(64 * h, 64 * (h + 1))
            total = jnp.sum(l_s[qb, rows], axis=1, keepdims=True)
            out_ref[0, qb, :, 128 * h : 128 * (h + 1)] = (acc_s[qb, rows] / total).astype(jnp.bfloat16)

    for s in range(16):
        found = pages[s]
        used = jnp.full((PAGE, 128), found, jnp.int32) > 0
        page = jnp.maximum(found - 1, 0)
        owner, half, n = page // 8, (page // 4) % 2, page % 4
        oy, oz, ox, oc = owner // 32, (owner // 8) % 4, (owner // 2) % 4, owner % 2
        for kv in range(2):
            rows = buf[half, oc, oy, ox, oz, kv, n]
            cache_ref[s, 0, :, 128 * kv : 128 * (kv + 1)] = jnp.where(used, rows, jnp.zeros_like(rows))

    def sent(ref, sem):
        remote(ref, ref, sem, z_recv.at[0], sibling).wait_send()

    sent(buf.at[:, 0, 0, 0, 0:3], z_send)
    sent(buf.at[0, 0, 0:3, 0:2], a_send)
    sent(buf.at[0, 0], b_send)
    sent(buf.at[0, 0, 0:2], f_send)
    sent(buf.at[0], d_send)
    sent(qbuf.at[:, 0:48], q_send)


def per_device(query_states, key_states, value_states, doc_lengths, page_slot):
    vmem = pl.BlockSpec(memory_space=pltpu.VMEM)
    smem = pl.BlockSpec(memory_space=pltpu.SMEM)
    dma = pltpu.SemaphoreType.DMA
    f32 = jnp.float32
    return pl.pallas_call(
        kernel,
        out_shape=(
            jax.ShapeDtypeStruct((1, 2, 64, 512), jnp.bfloat16),
            jax.ShapeDtypeStruct((16, 1, 16, 256), jnp.bfloat16),
        ),
        in_specs=[vmem, vmem, vmem, smem, vmem],
        out_specs=(vmem, vmem),
        scratch_shapes=[
            pltpu.VMEM((2, 2, 4, 4, 4, 2, 4, PAGE, 128), jnp.bfloat16),
            pltpu.VMEM((2, 64, 512), jnp.bfloat16),
            pltpu.VMEM((2, 256, 128), jnp.bfloat16),
            pltpu.VMEM((2, 256, 128), jnp.int32),
            pltpu.VMEM((2, 256, 128), jnp.int32),
            pltpu.VMEM((2, 256, 128), f32),
            pltpu.VMEM((2, 256, 128), f32),
            pltpu.VMEM((2, 256, 128), f32),
            pltpu.SMEM((16,), jnp.int32),
            dma((3,)),
            dma((2, 3)),
            dma((2, 4, 2)),
            dma((2, 4, 2)),
            dma((32,)),
            dma((3,)),
            dma(()), dma(()), dma(()), dma(()), dma(()), dma(()),
        ],
        compiler_params=pltpu.CompilerParams(
            collective_id=0, has_side_effects=True, vmem_limit_bytes=40 * 1024 * 1024
        ),
    )(query_states, key_states, value_states, doc_lengths, page_slot)


def solution(mesh):
    return jax.shard_map(
        per_device,
        mesh=mesh,
        in_specs=(
            P("blk", None, "head", None),
            P("blk", None, None, "head"),
            P("blk", None, None, "head"),
            P(),
            P(),
        ),
        out_specs=(P("blk", None, None, "head"), P("blk", "head", None, None)),
        check_vma=False,
    )
```

time: 595 us -> 60.3 us (0.10)
  waiting for transfers between devices: 397 us -> 0 us
  local copies, waits for them, and re-layouts: 105 us -> 3.73 us
  Pallas kernels: 0 us -> 55.3 us
  matrix products: 30.2 us -> 0 us
  other arithmetic: 27.7 us -> 0 us
  starting transfers between devices: 15.7 us -> 0 us
  between operations: 14.1 us -> 0.67 us
    all_gather x2 -> x0, waiting for transfers between devices: 385 us -> none  [the longest x1 206 us: per_device(): lax.all_gather(value_states, 'blk', axis=0, tiled=True)]
    pallas_call x0 -> x1, Pallas kernels: none -> 55.3 us  [per_device(): pl.pallas_call(kernel, out_shape=(jax.ShapeDtypeStruct((1, 2, 64, 512), j...]
    dynamic_slice x32 -> x0, local copies, waits for them, and re-layouts: 31.8 us -> none  [fold_groups(): lax.scan(visit_one, carried, (key_groups, value_groups, owner_ids))[0]]
    squeeze x32 -> x0, local copies, waits for them, and re-layouts: 31.7 us -> none  [fold_groups(): lax.scan(visit_one, carried, (key_groups, value_groups, owner_ids))[0]]
    dot_general x96 -> x0, matrix products: 30.2 us -> none  [the longest x32 14.1 us: attend_group(): jnp.einsum('qhk,kd->qhd', weights.astype(jnp.bfloat16), value_rows, prefe...]
    gather x32 -> x0, local copies, waits for them, and re-layouts: 18.3 us -> none  [place_pages(): jnp.take(page_slot, owner_ids, axis=0).reshape(-1) - my_index * slot_count]
    all_to_all x1 -> x0, starting transfers between devices: 15.6 us -> none  [per_device(): lax.all_to_all(query_states, 'head', split_axis=3, concat_axis=2, tiled=T...]
    all_to_all x1 -> x0, waiting for transfers between devices: 10.6 us -> none  [per_device(): lax.all_to_all(query_states, 'head', split_axis=3, concat_axis=2, tiled=T...]
  transfers between devices with their start and end apart: 3 -> 0, of which waited for: 3 -> 0; matrix products, arithmetic and copies ran while one was open for 1% -> 0% of each run, Pallas kernels for 0% -> 0%
where the time goes in v1:
time: 60.3 us; the launch traced here: 59.8 us
  Pallas kernels  55.3 us (92%)
  local copies, waits for them, and re-layouts  3.73 us (6%)
  between operations  0.67 us (1%)
    pallas_call x1, Pallas kernels, per_device(): pl.pallas_call(kernel, out_shape=(jax.ShapeDtypeStruct((1, 2, 64, 512), j...  55.3 us
    unnamed x11, local copies, waits for them, and re-layouts  3.73 us

profile of v1, /device:TPU:1, one launch (start us, length us, event | category | flops | bytes accessed | tf_op | source)
XLA Modules:
  0.0 59.8 jit_solution(17699120683842401941)
XLA Ops:
  0.6 0.0 copy-start.3
  0.6 0.0 copy-start
  0.6 0.9 %copy.7.slot_ref = s32[128,2,4]{2,1,0:T(2,128)S(1)} copy(s32[128,2,4]{0,2,1:T(4,128)} %param.9) | data formatting | bytes 8192 | tf_op args[4]
  1.5 0.0 copy-done.3
  1.5 0.0 copy-done
  1.6 0.0 copy-start.1
  1.6 0.8 %copy-done.1 = bf16[1,2,64,128]{3,2,1,0:T(8,128)(2,1)S(1)} copy-done((bf16[1,2,64,128]{3,2,1,0:T(8,128)(2,1)S(1)}, bf16[1,2,64,128]{3,2,1,0:T(8,128)(2,1)}, u32[]{:S(2)}) %copy-start.1) | copy-done | bytes 32792
  2.3 0.0 copy-start.2
  2.3 0.8 %copy-done.2 = bf16[1,2,64,128]{3,2,1,0:T(8,128)(2,1)S(1)} copy-done((bf16[1,2,64,128]{3,2,1,0:T(8,128)(2,1)S(1)}, bf16[1,2,64,128]{3,2,1,0:T(8,128)(2,1)}, u32[]{:S(2)}) %copy-start.2) | copy-done | bytes 32792
  3.1 55.3 %shard_map.68 = (bf16[1,2,64,512]{3,2,1,0:T(8,128)(2,1)S(1)}, bf16[16,1,16,256]{3,2,1,0:T(8,128)(2,1)S(1)}) custom-call(bf16[1,2,16,2048]{3,2,1,0:T(8,128)(2,1)S(1)} %copy-done, bf16[1,2,64,128]{3,2,1,0:T(8,128)(2,1)S(1)} %copy-done.1, bf16[1,2,64,128]{3,2,1,0:T(8,128)(2,1)S(1)} %copy-done.2, s32[3]{0:T(128)S(1)} %copy-done.3, s32[128,2,4]{2,1,0:T(2,128)S(1)} %copy.7.slot_ref), custom_call_target="tpu_custom_call" | custom-call | tf_op jit(solution)/shard_map/pallas_call | solution.py:258
  58.4 0.7 %copy.10 = bf16[1,2,64,512]{3,2,1,0:T(8,128)(2,1)} copy(bf16[1,2,64,512]{3,2,1,0:T(8,128)(2,1)S(1)} %get-tuple-element.4) | data formatting | bytes 262144
  59.1 0.7 %copy.11 = bf16[16,1,16,256]{3,2,1,0:T(8,128)(2,1)} copy(bf16[16,1,16,256]{3,2,1,0:T(8,128)(2,1)S(1)} %get-tuple-element.5) | data formatting | bytes 262144
Async XLA Ops:
  0.6 0.9 %copy-start.3 = (s32[3]{0:T(128)S(1)}, s32[3]{0:T(128)}, u32[]{:S(2)}) copy-start(s32[3]{0:T(128)} %doc_ref.1) | copy-start | bytes 40
  0.6 0.9 %copy-start = (bf16[1,2,16,2048]{3,2,1,0:T(8,128)(2,1)S(1)}, bf16[1,2,16,2048]{3,2,1,0:T(8,128)(2,1)}, u32[]{:S(2)}) copy-start(bf16[1,2,16,2048]{3,2,1,0:T(8,128)(2,1)} %q_ref.1) | copy-start | bytes 393220
  1.6 0.8 %copy-start.1 = (bf16[1,2,64,128]{3,2,1,0:T(8,128)(2,1)S(1)}, bf16[1,2,64,128]{3,2,1,0:T(8,128)(2,1)}, u32[]{:S(2)}) copy-start(bf16[1,2,64,128]{3,2,1,0:T(8,128)(2,1)} %k_ref.1) | copy-start | bytes 98308
  2.3 0.8 %copy-start.2 = (bf16[1,2,64,128]{3,2,1,0:T(8,128)(2,1)S(1)}, bf16[1,2,64,128]{3,2,1,0:T(8,128)(2,1)}, u32[]{:S(2)}) copy-start(bf16[1,2,64,128]{3,2,1,0:T(8,128)(2,1)} %v_ref.1) | copy-start | bytes 98308

commit v2 on v1

v2 whole, which is shorter than its diff:
```python
import functools
import jax
import jax.numpy as jnp
from jax import lax
from jax.experimental import pallas as pl
from jax.experimental.pallas import tpu as pltpu
from jax.sharding import PartitionSpec as P

MESH = pl.DeviceIdType.MESH
PAGE = 16
NEG = -1e30
LAG = 3
SEND = (3, 2, -1, -1)
NEED = (5, 4, 3, 3)
RATE = 2


def kernel(
    q_ref, k_ref, v_ref, doc_ref, slot_ref, out_ref, cache_ref,
    buf, qbuf, qrow, start, qpos, m_s, l_s, acc_s, pages,
    z_recv, a_recv, b_recv, f_recv, d_recv, q_recv, z_send, a_send, b_send, f_send, d_send, q_send,
    own_sem, go,
):
    blk = lax.axis_index("blk")
    head = lax.axis_index("head")
    y, z, x, c = blk // 32, (blk // 8) % 4, (blk // 2) % 4, blk % 2

    def device(yy, zz, xx, cc):
        return (((yy * 4 + zz) * 4 + xx) * 2 + cc, head)

    sibling = device(y, z, x, 1 - c)
    z_peers = [z + 1 - 2 * (z % 2), (z + 2) % 4, 3 - z]

    def remote(src, dst, send, recv, dev):
        return pltpu.make_async_remote_copy(
            src_ref=src, dst_ref=dst, send_sem=send, recv_sem=recv, device_id=dev, device_id_type=MESH
        )

    def signal(sem, dev):
        pl.semaphore_signal(sem, inc=1, device_id=dev, device_id_type=MESH)

    barrier = pltpu.get_barrier_semaphore()
    for d in range(1, 4):
        signal(barrier, device(y, z_peers[d - 1], x, 0))
        signal(barrier, device(y, z, (x + d) % 4, 0))
        signal(barrier, device((y + d) % 4, z, x, 0))
        signal(barrier, (blk + 1 - c, (head + d) % 4))

    @pl.when(c == 1)
    def _():
        signal(barrier, sibling)

    own = []
    for half in range(2):
        own.append(pltpu.make_async_copy(k_ref.at[half], buf.at[half, c, y, x, z, 0], own_sem.at[2 * half]))
        own.append(pltpu.make_async_copy(v_ref.at[half], buf.at[half, c, y, x, z, 1], own_sem.at[2 * half + 1]))
    own.append(
        pltpu.make_async_copy(
            q_ref.at[0, :, :, pl.ds(pl.multiple_of(head * 512, 512), 512)],
            qbuf.at[:, pl.ds(pl.multiple_of(head * 16, 16), 16), :],
            own_sem.at[4],
        )
    )
    for copy in own:
        copy.start()

    for copy in own:
        copy.wait()

    @pl.when(c == 0)
    def _():
        pl.semaphore_wait(barrier, 19)
        signal(go.at[0], sibling)

    @pl.when(c == 1)
    def _():
        pl.semaphore_wait(go.at[0], 1)

    def query_copy(d):
        to = (head + d) % 4
        return remote(
            q_ref.at[0, :, :, pl.ds(pl.multiple_of(to * 512, 512), 512)],
            qbuf.at[:, pl.ds(pl.multiple_of(head * 16, 16), 16), :],
            q_send, q_recv.at[d - 1], (blk, to),
        )

    def send_queries():
        @pl.when(c == 1)
        def _():
            pl.semaphore_wait(barrier, 6)
            signal(go.at[1], sibling)

        @pl.when(c == 0)
        def _():
            pl.semaphore_wait(go.at[1], 1)

        for d in range(1, 4):
            query_copy(d).start()

    def slice_z(s):
        return (z + 4 + s * (1 - 2 * (z % 2)) * (s % 2) + 2 * (s // 2) * (1 - 2 * (z // 2)) - (s // 3) * 2 * (1 - 2 * (z % 2))) % 4

    def row(half, core, off, zz):
        if half == 0:
            return buf.at[0, core, (y + off) % 4, :, zz]
        return buf.at[1, core, :, (x + off) % 4, zz]

    def part(half, off, zz, kv):
        if half == 0:
            return buf.at[0, c, (y + off) % 4, :, zz, kv]
        return buf.at[1, c, :, (x + off) % 4, zz, kv]

    def second_device(half, step):
        return device((y + step) % 4, z, x, c) if half == 0 else device(y, z, (x + step) % 4, c)

    def to_sibling(half, off, s):
        ref = row(half, c, off, slice_z(s))
        remote(ref, ref, d_send, d_recv.at[s], sibling).start()

    def send_z():
        for d in range(3):
            unit = buf.at[:, c, y, x, z]
            remote(unit, unit, z_send, z_recv.at[d], device(y, z_peers[d], x, c)).start()

    def first_axis(s):
        zz = slice_z(s)
        if not isinstance(s, int):
            unit = buf.at[:, c, y, x, zz]
            remote(unit, unit, z_send, z_recv.at[s - 1], sibling).wait_recv()
        low = buf.at[0, c, y, x, zz]
        high = buf.at[1, c, y, x, zz]
        for d in (1, 3, 2):
            remote(low, low, a_send, a_recv.at[0, s], device(y, z, (x + d) % 4, c)).start()
            remote(high, high, a_send, a_recv.at[1, s], device((y + d) % 4, z, x, c)).start()

    def second_axis(s):
        for half in range(2):
            three = buf.at[0, 0, 0, 0, 0:3]
            remote(three, three, a_send, a_recv.at[half, s], sibling).wait_recv()
            own_row = row(half, c, 0, slice_z(s))
            for direction in range(2):
                remote(
                    own_row, own_row, b_send, b_recv.at[half, s, direction], second_device(half, (1, 3)[direction])
                ).start()
            to_sibling(half, 0, s)

    def forward(s):
        zz = slice_z(s)
        for direction in (1, 0):
            for half in range(2):
                off = (3, 1)[direction]
                got = row(half, c, off, zz)
                remote(got, got, b_send, b_recv.at[half, s, direction], sibling).wait_recv()
                piece = part(half, off, zz, direction)
                remote(piece, piece, f_send, f_recv.at[half, s], second_device(half, (1, 3)[direction])).start()
                to_sibling(half, off, s)

    def far(s):
        for half in range(2):
            got = row(half, c, 2, slice_z(s))
            remote(got, got, f_send, f_recv.at[half, s], sibling).wait_recv()
            to_sibling(half, 2, s)

    send_z()
    first_axis(0)

    @pl.when(head >= 2)
    def _():
        send_queries()


    bound0 = doc_ref[0]
    bound1 = doc_ref[0] + doc_ref[1]
    for qb in range(2):
        token = lax.broadcasted_iota(jnp.int32, (256, 128), 0) % 64
        pos = token + (blk if qb == 0 else 255 - blk) * 64
        qpos[qb] = pos
        start[qb] = jnp.where(pos >= bound1, bound1, jnp.where(pos >= bound0, bound0, 0))
    m_s[...] = jnp.full_like(m_s, NEG)
    l_s[...] = jnp.zeros_like(l_s)
    acc_s[...] = jnp.zeros_like(acc_s)

    local = slot_ref[...] - blk * 16
    ident = (
        lax.broadcasted_iota(jnp.int32, local.shape, 0) * 4
        + lax.broadcasted_iota(jnp.int32, local.shape, 1)
        + lax.broadcasted_iota(jnp.int32, local.shape, 2) * 8
        + 1
    )
    for s in range(16):
        pages[s] = jnp.max(jnp.where(local == s, ident, 0))

    scale = 128 ** -0.5 * 1.4426950408889634

    def attend(s):
        zz = slice_z(s)

        @functools.cache
        def block(i):
            after = lax.div(i + 8 - (y + 1), 8)
            high = lax.div(i + 8 - (y + 5), 8)
            yy = i - after * (y + 1) - high * (4 - y)
            return after, high, yy

        def scores_of(i):
            qb, half, yy = block(i)
            keys = buf[half, :, yy, :, zz, 0].reshape(512, 128)
            return lax.dot_general(qrow[qb], keys, (((1,), (1,)), ((), ())), preferred_element_type=jnp.float32)

        lane = lax.broadcasted_iota(jnp.int32, (1, 128), 1)
        ahead = scores_of(0)
        for i in range(9):
            scores = ahead
            if i < 8:
                ahead = scores_of(i + 1)
            qb, half, yy = block(i)
            sign = 1 - 2 * half
            first = half * 255 + sign * (32 * yy + 8 * zz)
            lo, hi = start[qb], qpos[qb]
            parts = []
            for t in range(4):
                unit = t // 2 + 2 * (2 * (t % 2) + lane // 64)
                k_pos = (first + sign * unit) * 64 + lane % 64
                piece = scores[:, 128 * t : 128 * (t + 1)]
                parts.append(jnp.where((k_pos >= lo) & (k_pos <= hi), piece, NEG))
            top = jnp.maximum(jnp.maximum(parts[0], parts[1]), jnp.maximum(parts[2], parts[3]))
            old = m_s[qb]
            new = jnp.maximum(old, jnp.max(top, axis=1, keepdims=True))
            m_s[qb] = new
            factor = jnp.exp2((old - new) * scale)
            weights = [jnp.exp2((piece - new) * scale) for piece in parts]
            l_s[qb] = l_s[qb] * factor + ((weights[0] + weights[1]) + (weights[2] + weights[3]))
            rounded = jnp.concatenate([w.astype(jnp.bfloat16) for w in weights], axis=1)
            values = buf[half, :, yy, :, zz, 1].reshape(512, 128)
            acc_s[qb] = acc_s[qb] * factor + jnp.dot(rounded, values, preferred_element_type=jnp.float32)

    def compute(s, _):
        whole = buf.at[:, 0, :, :, 0]
        remote(whole, whole, d_send, d_recv.at[s], sibling).wait_recv()
        attend(s)
        return 0

    def by_head(table):
        return table[3] + (table[0] - table[3]) * (1 - (head + 3) // 4) + (table[1] - table[3]) * (head % 3 % 2)

    send_at, need_at = by_head(SEND), by_head(NEED)

    def computed(w):
        return jnp.clip(jnp.minimum(w - LAG, RATE * (w + 1 - need_at)), 0, 4)

    def steps(w, _):
        @pl.when(w < 5)
        def _():
            second_axis(w - 1)

        @pl.when(w < 4)
        def _():
            first_axis(w)

        @pl.when(w == send_at)
        def _():
            send_queries()

        @pl.when((w >= 2) & (w < 6))
        def _():
            forward(w - 2)

        @pl.when((w >= 3) & (w < 7))
        def _():
            far(w - 3)

        @pl.when(w == need_at)
        def _():
            for d in range(1, 4):
                query_copy(d).wait_recv()
            for qb in range(2):
                for h in range(4):
                    qrow[qb, 64 * h : 64 * (h + 1)] = qbuf[qb, :, 128 * h : 128 * (h + 1)]

        lax.fori_loop(computed(w - 1), computed(w), compute, 0)
        return 0

    lax.fori_loop(1, 8, steps, 0)

    for qb in range(2):
        for h in range(4):
            rows = slice(64 * h, 64 * (h + 1))
            total = jnp.sum(l_s[qb, rows], axis=1, keepdims=True)
            out_ref[0, qb, :, 128 * h : 128 * (h + 1)] = (acc_s[qb, rows] / total).astype(jnp.bfloat16)

    for s in range(16):
        found = pages[s]
        used = jnp.full((PAGE, 128), found, jnp.int32) > 0
        page = jnp.maximum(found - 1, 0)
        owner, half, n = page // 8, (page // 4) % 2, page % 4
        oy, oz, ox, oc = owner // 32, (owner // 8) % 4, (owner // 2) % 4, owner % 2
        for kv in range(2):
            rows = buf[half, oc, oy, ox, oz, kv, n]
            cache_ref[s, 0, :, 128 * kv : 128 * (kv + 1)] = jnp.where(used, rows, jnp.zeros_like(rows))

    def sent(ref, sem):
        remote(ref, ref, sem, z_recv.at[0], sibling).wait_send()

    sent(buf.at[:, 0, 0, 0, 0:3], z_send)
    sent(buf.at[0, 0, 0:3, 0:2], a_send)
    sent(buf.at[0, 0], b_send)
    sent(buf.at[0, 0, 0:2], f_send)
    sent(buf.at[0], d_send)
    sent(qbuf.at[:, 0:48], q_send)


def per_device(query_states, key_states, value_states, doc_lengths, page_slot):
    vmem = pl.BlockSpec(memory_space=pltpu.VMEM)
    hbm = pl.BlockSpec(memory_space=pltpu.HBM)
    smem = pl.BlockSpec(memory_space=pltpu.SMEM)
    dma = pltpu.SemaphoreType.DMA
    f32 = jnp.float32
    return pl.pallas_call(
        kernel,
        out_shape=(
            jax.ShapeDtypeStruct((1, 2, 64, 512), jnp.bfloat16),
            jax.ShapeDtypeStruct((16, 1, 16, 256), jnp.bfloat16),
        ),
        in_specs=[hbm, hbm, hbm, smem, vmem],
        out_specs=(vmem, vmem),
        scratch_shapes=[
            pltpu.VMEM((2, 2, 4, 4, 4, 2, 4, PAGE, 128), jnp.bfloat16),
            pltpu.VMEM((2, 64, 512), jnp.bfloat16),
            pltpu.VMEM((2, 256, 128), jnp.bfloat16),
            pltpu.VMEM((2, 256, 128), jnp.int32),
            pltpu.VMEM((2, 256, 128), jnp.int32),
            pltpu.VMEM((2, 256, 128), f32),
            pltpu.VMEM((2, 256, 128), f32),
            pltpu.VMEM((2, 256, 128), f32),
            pltpu.SMEM((16,), jnp.int32),
            dma((3,)),
            dma((2, 4)),
            dma((2, 4, 2)),
            dma((2, 4)),
            dma((4,)),
            dma((3,)),
            dma(()), dma(()), dma(()), dma(()), dma(()), dma(()),
            dma((5,)),
            pltpu.SemaphoreType.REGULAR((2,)),
        ],
        compiler_params=pltpu.CompilerParams(
            collective_id=0, has_side_effects=True, vmem_limit_bytes=62 * 1024 * 1024
        ),
    )(
        query_states,
        key_states.reshape(2, 4, PAGE, 128),
        value_states.reshape(2, 4, PAGE, 128),
        doc_lengths,
        page_slot.transpose(1, 2, 0),
    )


def solution(mesh):
    return jax.shard_map(
        per_device,
        mesh=mesh,
        in_specs=(
            P("blk", None, "head", None),
            P("blk", None, None, "head"),
            P("blk", None, None, "head"),
            P(),
            P(),
        ),
        out_specs=(P("blk", None, None, "head"), P("blk", "head", None, None)),
        check_vma=False,
    )
```

time: 60.3 us -> 52.9 us (0.88)
  Pallas kernels: 55.3 us -> 49.8 us
  local copies, waits for them, and re-layouts: 3.73 us -> 2.26 us
    pallas_call x1, Pallas kernels: 55.3 us -> 49.8 us  [per_device(): pl.pallas_call(kernel, out_shape=(jax.ShapeDtypeStruct((1, 2, 64, 512), j...]
    unnamed x11 -> x4, local copies, waits for them, and re-layouts: 3.73 us -> 2.26 us
where the time goes in v2:
time: 52.9 us; the launch traced here: 52.7 us
  Pallas kernels  49.8 us (94%)
  local copies, waits for them, and re-layouts  2.26 us (4%)
  between operations  0.65 us (1%)
    pallas_call x1, Pallas kernels, per_device(): pl.pallas_call(kernel, out_shape=(jax.ShapeDtypeStruct((1, 2, 64, 512), j...  49.8 us
    unnamed x4, local copies, waits for them, and re-layouts  2.26 us

profile of v2, /device:TPU:1, one launch (start us, length us, event | category | flops | bytes accessed | tf_op | source)
XLA Modules:
  0.0 52.7 jit_solution(7114741053635272239)
XLA Ops:
  0.6 49.8 %shard_map.68 = (bf16[1,2,64,512]{3,2,1,0:T(8,128)(2,1)}, bf16[16,1,16,256]{3,2,1,0:T(8,128)(2,1)}) custom-call(bf16[1,2,16,2048]{3,2,1,0:T(8,128)(2,1)} %q_ref.1, bf16[2,4,16,128]{3,2,1,0:T(8,128)(2,1)} %bitcast.3, bf16[2,4,16,128]{3,2,1,0:T(8,128)(2,1)} %bitcast.4, s32[3]{0:T(128)} %doc_ref.1, s32[2,4,128]{2,1,0:T(4,128)} %bitcast.5), custom_call_target="tpu_custom_call" | custom-call | tf_op jit(solution)/shard_map/pallas_call | solution.py:318
  50.4 0.0 copy-start
  50.4 1.6 %copy.9 = bf16[1,2,64,512]{3,2,1,0:T(8,128)(2,1)} copy(bf16[1,2,64,512]{3,2,1,0:T(8,128)(2,1)} %get-tuple-element.4) | data formatting | bytes 262144
  52.0 0.0 copy-done
  52.0 0.7 %copy.10 = bf16[16,1,16,256]{3,2,1,0:T(8,128)(2,1)} copy(bf16[16,1,16,256]{3,2,1,0:T(8,128)(2,1)S(1)} %copy-done) | data formatting | bytes 262144
Async XLA Ops:
  50.4 1.6 %copy-start = (bf16[16,1,16,256]{3,2,1,0:T(8,128)(2,1)S(1)}, bf16[16,1,16,256]{3,2,1,0:T(8,128)(2,1)}, u32[]{:S(2)}) copy-start(bf16[16,1,16,256]{3,2,1,0:T(8,128)(2,1)} %get-tuple-element.5) | copy-start | bytes 393220

commit v3 on v2

--- a/solution.py
+++ b/solution.py
@@ -9,9 +9,18 @@
 MESH = pl.DeviceIdType.MESH
 PAGE = 16
 NEG = -1e30
-LAG = 3
-SEND = (3, 2, -1, -1)
-NEED = (5, 4, 3, 3)
+PLAN = (
+    (("A", 1), ("B", 0),),
+    (("A", 2), ("B", 1), ("F", 0),),
+    (("A", 3), ("B", 2), ("F", 1), ("R", 0),),
+    (("B", 3), ("F", 2), ("R", 1),),
+    (("F", 3), ("R", 2),),
+    (("R", 3),),
+    (),
+)
+READY = (2, 3, 4, 6)
+SEND = (2, 1, -1, -1)
+NEED = (4, 3, 2, 2)
 RATE = 2
 
 
@@ -29,7 +38,6 @@
         return (((yy * 4 + zz) * 4 + xx) * 2 + cc, head)
 
     sibling = device(y, z, x, 1 - c)
-    z_peers = [z + 1 - 2 * (z % 2), (z + 2) % 4, 3 - z]
 
     def remote(src, dst, send, recv, dev):
         return pltpu.make_async_remote_copy(
@@ -41,10 +49,17 @@
 
     barrier = pltpu.get_barrier_semaphore()
     for d in range(1, 4):
-        signal(barrier, device(y, z_peers[d - 1], x, 0))
         signal(barrier, device(y, z, (x + d) % 4, 0))
         signal(barrier, device((y + d) % 4, z, x, 0))
         signal(barrier, (blk + 1 - c, (head + d) % 4))
+
+    inner = lax.rem(lax.div(z + 1, 2), 2)
+    up = 1 - 2 * lax.div(z, 2)
+    signal(barrier, device(y, z + up * (1 - 2 * inner), x, 0))
+
+    @pl.when(inner == 1)
+    def _():
+        signal(barrier, device(y, z + up, x, 0))
 
     @pl.when(c == 1)
     def _():
@@ -69,7 +84,7 @@
 
     @pl.when(c == 0)
     def _():
-        pl.semaphore_wait(barrier, 19)
+        pl.semaphore_wait(barrier, 15 + 2 * inner)
         signal(go.at[0], sibling)
 
     @pl.when(c == 1)
@@ -98,7 +113,10 @@
             query_copy(d).start()
 
     def slice_z(s):
-        return (z + 4 + s * (1 - 2 * (z % 2)) * (s % 2) + 2 * (s // 2) * (1 - 2 * (z // 2)) - (s // 3) * 2 * (1 - 2 * (z % 2))) % 4
+        first = 1 - lax.div(s + 3, 4) if not isinstance(s, int) else int(s == 0)
+        second = (lax.div(s + 3, 4) - lax.div(s + 2, 4)) if not isinstance(s, int) else int(s == 1)
+        step = s + inner * (first - second)
+        return (1 - lax.div(z, 2)) * step + lax.div(z, 2) * (3 - step)
 
     def row(half, core, off, zz):
         if half == 0:
@@ -117,16 +135,35 @@
         ref = row(half, c, off, slice_z(s))
         remote(ref, ref, d_send, d_recv.at[s], sibling).start()
 
+    def z_copy(unit, place, zz):
+        return remote(unit, unit, z_send, z_recv.at[place - 1], device(y, zz, x, c))
+
     def send_z():
-        for d in range(3):
-            unit = buf.at[:, c, y, x, z]
-            remote(unit, unit, z_send, z_recv.at[d], device(y, z_peers[d], x, c)).start()
+        unit = buf.at[:, c, y, x, z]
+
+        @pl.when(inner == 0)
+        def _():
+            z_copy(unit, 1, z + up).start()
+
+        @pl.when(inner == 1)
+        def _():
+            z_copy(unit, 1, z - up).start()
+            z_copy(unit, 2, z + up).start()
 
     def first_axis(s):
         zz = slice_z(s)
-        if not isinstance(s, int):
+        if s > 0:
             unit = buf.at[:, c, y, x, zz]
             remote(unit, unit, z_send, z_recv.at[s - 1], sibling).wait_recv()
+
+            @pl.when(inner == (1 if s == 1 else 2))
+            def _():
+                z_copy(unit, 3, z + up).start()
+
+            @pl.when(inner == (1 if s > 1 else 2))
+            def _():
+                remote(unit, unit, z_send, z_recv.at[s - 1], device(y, z - up, x, c)).start()
+
         low = buf.at[0, c, y, x, zz]
         high = buf.at[1, c, y, x, zz]
         for d in (1, 3, 2):
@@ -137,23 +174,31 @@
         for half in range(2):
             three = buf.at[0, 0, 0, 0, 0:3]
             remote(three, three, a_send, a_recv.at[half, s], sibling).wait_recv()
-            own_row = row(half, c, 0, slice_z(s))
-            for direction in range(2):
-                remote(
-                    own_row, own_row, b_send, b_recv.at[half, s, direction], second_device(half, (1, 3)[direction])
-                ).start()
+            for first in range(2):
+                for direction in range(2):
+                    kv = direction if first == 0 else 1 - direction
+                    piece = part(half, 0, slice_z(s), kv)
+                    remote(
+                        piece, piece, b_send, b_recv.at[half, s, direction, kv], second_device(half, (1, 3)[direction])
+                    ).start()
             to_sibling(half, 0, s)
 
     def forward(s):
         zz = slice_z(s)
+
+        def near(half, direction, kv):
+            piece = part(half, (3, 1)[direction], zz, kv)
+            remote(piece, piece, b_send, b_recv.at[half, s, direction, kv], sibling).wait_recv()
+            return piece
+
         for direction in (1, 0):
             for half in range(2):
-                off = (3, 1)[direction]
-                got = row(half, c, off, zz)
-                remote(got, got, b_send, b_recv.at[half, s, direction], sibling).wait_recv()
-                piece = part(half, off, zz, direction)
+                piece = near(half, direction, direction)
                 remote(piece, piece, f_send, f_recv.at[half, s], second_device(half, (1, 3)[direction])).start()
-                to_sibling(half, off, s)
+        for direction in (1, 0):
+            for half in range(2):
+                near(half, direction, 1 - direction)
+                to_sibling(half, (3, 1)[direction], s)
 
     def far(s):
         for half in range(2):
@@ -246,28 +291,21 @@
     send_at, need_at = by_head(SEND), by_head(NEED)
 
     def computed(w):
-        return jnp.clip(jnp.minimum(w - LAG, RATE * (w + 1 - need_at)), 0, 4)
+        ready = sum(lax.div(w + 16 - at, 16) for at in READY)
+        return jnp.clip(jnp.minimum(ready, RATE * (w + 1 - need_at)), 0, 4)
 
     def steps(w, _):
-        @pl.when(w < 5)
-        def _():
-            second_axis(w - 1)
-
-        @pl.when(w < 4)
-        def _():
-            first_axis(w)
+        for at, list_of in enumerate(PLAN):
+            if list_of:
+
+                @pl.when(w == at)
+                def _(list_of=list_of):
+                    for kind, s in list_of:
+                        {"A": first_axis, "B": second_axis, "F": forward, "R": far}[kind](s)
 
         @pl.when(w == send_at)
         def _():
             send_queries()
-
-        @pl.when((w >= 2) & (w < 6))
-        def _():
-            forward(w - 2)
-
-        @pl.when((w >= 3) & (w < 7))
-        def _():
-            far(w - 3)
 
         @pl.when(w == need_at)
         def _():
@@ -280,7 +318,7 @@
         lax.fori_loop(computed(w - 1), computed(w), compute, 0)
         return 0
 
-    lax.fori_loop(1, 8, steps, 0)
+    lax.fori_loop(0, len(PLAN), steps, 0)
 
     for qb in range(2):
         for h in range(4):
@@ -301,7 +339,12 @@
     def sent(ref, sem):
         remote(ref, ref, sem, z_recv.at[0], sibling).wait_send()
 
-    sent(buf.at[:, 0, 0, 0, 0:3], z_send)
+    sent(buf.at[:, 0, 0, 0, 0:1], z_send)
+
+    @pl.when(inner == 1)
+    def _():
+        sent(buf.at[:, 0, 0, 0, 0:4], z_send)
+
     sent(buf.at[0, 0, 0:3, 0:2], a_send)
     sent(buf.at[0, 0], b_send)
     sent(buf.at[0, 0, 0:2], f_send)
@@ -335,7 +378,7 @@
             pltpu.SMEM((16,), jnp.int32),
             dma((3,)),
             dma((2, 4)),
-            dma((2, 4, 2)),
+            dma((2, 4, 2, 2)),
             dma((2, 4)),
             dma((4,)),
             dma((3,)),

time: 52.9 us -> 48.8 us (0.922)
  Pallas kernels: 49.8 us -> 45.1 us
    pallas_call x1, Pallas kernels: 49.8 us -> 45.1 us  [per_device(): pl.pallas_call(kernel, out_shape=(jax.ShapeDtypeStruct((1, 2, 64, 512), j...]
where the time goes in v3:
time: 48.8 us; the launch traced here: 48.1 us
  Pallas kernels  45.1 us (92%)
  local copies, waits for them, and re-layouts  2.26 us (5%)
  between operations  0.65 us (1%)
    pallas_call x1, Pallas kernels, per_device(): pl.pallas_call(kernel, out_shape=(jax.ShapeDtypeStruct((1, 2, 64, 512), j...  45.1 us
    unnamed x4, local copies, waits for them, and re-layouts  2.26 us

profile of v3, /device:TPU:1, one launch (start us, length us, event | category | flops | bytes accessed | tf_op | source)
XLA Modules:
  0.0 48.1 jit_solution(1621028090930271980)
XLA Ops:
  0.6 45.1 %shard_map.68 = (bf16[1,2,64,512]{3,2,1,0:T(8,128)(2,1)}, bf16[16,1,16,256]{3,2,1,0:T(8,128)(2,1)}) custom-call(bf16[1,2,16,2048]{3,2,1,0:T(8,128)(2,1)} %q_ref.1, bf16[2,4,16,128]{3,2,1,0:T(8,128)(2,1)} %bitcast.3, bf16[2,4,16,128]{3,2,1,0:T(8,128)(2,1)} %bitcast.4, s32[3]{0:T(128)} %doc_ref.1, s32[2,4,128]{2,1,0:T(4,128)} %bitcast.5), custom_call_target="tpu_custom_call" | custom-call | tf_op jit(solution)/shard_map/pallas_call | solution.py:361
  45.8 0.0 copy-start
  45.8 1.6 %copy.9 = bf16[1,2,64,512]{3,2,1,0:T(8,128)(2,1)} copy(bf16[1,2,64,512]{3,2,1,0:T(8,128)(2,1)} %get-tuple-element.4) | data formatting | bytes 262144
  47.4 0.0 copy-done
  47.4 0.7 %copy.10 = bf16[16,1,16,256]{3,2,1,0:T(8,128)(2,1)} copy(bf16[16,1,16,256]{3,2,1,0:T(8,128)(2,1)S(1)} %copy-done) | data formatting | bytes 262144
Async XLA Ops:
  45.8 1.6 %copy-start = (bf16[16,1,16,256]{3,2,1,0:T(8,128)(2,1)S(1)}, bf16[16,1,16,256]{3,2,1,0:T(8,128)(2,1)}, u32[]{:S(2)}) copy-start(bf16[16,1,16,256]{3,2,1,0:T(8,128)(2,1)} %get-tuple-element.5) | copy-start | bytes 393220

commit v4 on v3

--- a/solution.py
+++ b/solution.py
@@ -18,9 +18,9 @@
     (("R", 3),),
     (),
 )
-READY = (2, 3, 4, 6)
+READY = (3, 4, 5, 6)
 SEND = (2, 1, -1, -1)
-NEED = (4, 3, 2, 2)
+NEED = (3, 3, 3, 3)
 RATE = 2
 
 

time: 48.8 us -> 47.6 us (0.975)
  Pallas kernels: 45.1 us -> 44.4 us
    pallas_call x1, Pallas kernels: 45.1 us -> 44.4 us  [per_device(): pl.pallas_call(kernel, out_shape=(jax.ShapeDtypeStruct((1, 2, 64, 512), j...]
where the time goes in v4:
time: 47.6 us; the launch traced here: 47.3 us
  Pallas kernels  44.4 us (93%)
  local copies, waits for them, and re-layouts  2.26 us (5%)
  between operations  0.65 us (1%)
    pallas_call x1, Pallas kernels, per_device(): pl.pallas_call(kernel, out_shape=(jax.ShapeDtypeStruct((1, 2, 64, 512), j...  44.4 us
    unnamed x4, local copies, waits for them, and re-layouts  2.26 us

profile of v4, /device:TPU:1, one launch (start us, length us, event | category | flops | bytes accessed | tf_op | source)
XLA Modules:
  0.0 47.3 jit_solution(13983864121347860436)
XLA Ops:
  0.6 44.4 %shard_map.68 = (bf16[1,2,64,512]{3,2,1,0:T(8,128)(2,1)}, bf16[16,1,16,256]{3,2,1,0:T(8,128)(2,1)}) custom-call(bf16[1,2,16,2048]{3,2,1,0:T(8,128)(2,1)} %q_ref.1, bf16[2,4,16,128]{3,2,1,0:T(8,128)(2,1)} %bitcast.3, bf16[2,4,16,128]{3,2,1,0:T(8,128)(2,1)} %bitcast.4, s32[3]{0:T(128)} %doc_ref.1, s32[2,4,128]{2,1,0:T(4,128)} %bitcast.5), custom_call_target="tpu_custom_call" | custom-call | tf_op jit(solution)/shard_map/pallas_call | solution.py:361
  45.1 0.0 copy-start
  45.1 1.6 %copy.9 = bf16[1,2,64,512]{3,2,1,0:T(8,128)(2,1)} copy(bf16[1,2,64,512]{3,2,1,0:T(8,128)(2,1)} %get-tuple-element.4) | data formatting | bytes 262144
  46.7 0.0 copy-done
  46.7 0.7 %copy.10 = bf16[16,1,16,256]{3,2,1,0:T(8,128)(2,1)} copy(bf16[16,1,16,256]{3,2,1,0:T(8,128)(2,1)S(1)} %copy-done) | data formatting | bytes 262144
Async XLA Ops:
  45.1 1.6 %copy-start = (bf16[16,1,16,256]{3,2,1,0:T(8,128)(2,1)S(1)}, bf16[16,1,16,256]{3,2,1,0:T(8,128)(2,1)}, u32[]{:S(2)}) copy-start(bf16[16,1,16,256]{3,2,1,0:T(8,128)(2,1)} %get-tuple-element.5) | copy-start | bytes 393220
